TPU v7x, 512 devices: a whole 4x4x16 slice. The times are simulated.
512 devices in a mesh: segment: 16 (over z_lo, x), dp: 8 (over y, core), mp: 4 (over z_hi).
Axes of the slice: x: 4, y: 4, z: 16 (z_hi: 4, z_lo: 4; z = z_hi * 4 + z_lo), core: 2. Of those that a mesh axis runs over, the one named last changes fastest.
Arguments:
- encoder_image_states: bfloat16 [8, 128, 8192], P('dp', 'segment'), may hold values from -6 to 6
- frozen_key_value: bfloat16 [16, 8192, 2, 1024], P('segment', 'dp', None, 'mp'), may hold values from -0.0625 to 0.0625
- adapter_down_weight: bfloat16 [16, 8192, 128], P('segment', 'mp'), may hold values from -0.0625 to 0.0625
- adapter_up_weight: bfloat16 [16, 2, 64, 1024], P('segment', None, None, 'mp'), may hold values from -0.75 to 0.75
- queries: bfloat16 [16, 8, 128, 8192], P('segment', 'dp', None, 'mp'), may hold values from -9 to 9
- cotangent: bfloat16 [16, 8, 128, 8192], P('segment', 'dp', None, 'mp'), may hold values from -1.5 to 1.5
- text_token_length: int32 [8], P('dp'), may hold values from 32 to 128
- image_tile_count: int32 [8], P('dp'), may hold values from 1 to 4
Outputs:
- grad_down: bfloat16 [16, 8192, 128], P('segment', 'mp')
- up_gradient: bfloat16 [16, 2, 64, 1024], P('segment', None, None, 'mp')
- grad_image: float32 [8, 128, 8192], P('dp', 'segment')
All inputs are finite; a program needn't handle non-finite values.
Results may differ from a plain program's by a relative error of at most 0.017.
The roundings to bfloat16 on the way count: a program that leaves them out, or rounds other values in their place, can miss the bound.
Values may be sent and summed in bfloat16 or wider, within the bound.
No kernel may reach another device: no remote copies, remote signals or barrier semaphores. Data moves between devices by JAX's collectives and lax.ppermute only.
A program may use at most 64 MiB of HBM per device.

v0:
```python
import jax
import jax.numpy as jnp
from jax import lax
from jax.sharding import PartitionSpec as P

HD = 128
TILES = 4
adapter_scale = 2.0
contract_rows = (((0,), (0,)), ((), ()))
contracted_columns = (((1,), (1,)), ((), ()))


def body(
    encoder_image_states,
    frozen_key_value,
    adapter_down_weight,
    adapter_up_weight,
    queries,
    cotangent,
    text_token_length,
    image_tile_count,
):
    samples = encoder_image_states.shape[0]
    model_width = encoder_image_states.shape[2]
    whole_img = lax.all_gather(encoder_image_states, "segment", axis=1, tiled=True)
    image_rows = whole_img.shape[1]
    flat_rows = samples * image_rows
    flat_img = whole_img.reshape(flat_rows, model_width)
    fourth_part = adapter_down_weight.shape[1]
    parallel_index = lax.axis_index("mp")
    image_fourth = lax.dynamic_slice_in_dim(flat_img, parallel_index * fourth_part, fourth_part, 1)
    lowrank_state = adapter_up_weight.shape[2]
    key_value_columns = adapter_up_weight.shape[3]
    lowrank_projection = lax.psum(
        jnp.dot(image_fourth, adapter_down_weight[0], preferred_element_type=jnp.float32), "mp"
    ).astype(jnp.bfloat16)
    adapted_weight = jnp.concatenate(
        [
            jnp.dot(
                lowrank_projection[:, :lowrank_state],
                adapter_up_weight[0, 0],
                preferred_element_type=jnp.float32,
            ),
            jnp.dot(
                lowrank_projection[:, lowrank_state:],
                adapter_up_weight[0, 1],
                preferred_element_type=jnp.float32,
            ),
        ],
        axis=1,
    )
    local_weight = frozen_key_value[0]
    full_weight = lax.all_gather(local_weight, "dp", axis=0, tiled=True).reshape(
        model_width, 2 * key_value_columns
    )
    frozen_output = jnp.dot(flat_img, full_weight, preferred_element_type=jnp.float32)
    key_value_pair = (frozen_output + adapter_scale * adapted_weight).astype(jnp.bfloat16)
    local_heads = queries.shape[3] // HD
    local_kv = key_value_columns // HD
    group_size = local_heads // local_kv
    text_rows = queries.shape[2]
    query_rows = queries[0].reshape(samples, text_rows, local_kv, group_size, HD)
    cot_rows = cotangent[0].reshape(samples, text_rows, local_kv, group_size, HD)
    key_rows = key_value_pair[:, :key_value_columns].reshape(samples, image_rows, local_kv, HD)
    value_rows = key_value_pair[:, key_value_columns:].reshape(samples, image_rows, local_kv, HD)
    key_mask = jnp.arange(image_rows, dtype=jnp.int32)[None, :] < image_tile_count[:, None] * (
        image_rows // TILES
    )
    row_mask = (
        jnp.arange(text_rows, dtype=jnp.int32)[None, :] < text_token_length[:, None]
    ).astype(jnp.float32)
    scores = jnp.einsum(
        "btgrd,bjgd->bgrtj", query_rows, key_rows, preferred_element_type=jnp.float32
    ) * HD ** (-0.5)
    masked = jnp.where(key_mask[:, None, None, None, :], scores, -1e30)
    row_top = jnp.max(masked, axis=-1, keepdims=True)
    shifted = jnp.exp(masked - row_top)
    attention = shifted / jnp.sum(shifted, axis=-1, keepdims=True)
    row_gate = row_mask[:, None, None, :, None]
    kept = attention.astype(jnp.bfloat16) * row_gate.astype(jnp.bfloat16)
    dweights = jnp.einsum(
        "btgrd,bjgd->bgrtj", cot_rows, value_rows, preferred_element_type=jnp.float32
    )
    row_delta = jnp.sum(attention * dweights, axis=-1, keepdims=True)
    dscore = (attention * (dweights - row_delta) * row_gate * HD ** (-0.5)).astype(jnp.bfloat16)
    key_grad = jnp.einsum(
        "bgrtj,btgrd->bjgd", dscore, query_rows, preferred_element_type=jnp.float32
    )
    value_grad = jnp.einsum("bgrtj,btgrd->bjgd", kept, cot_rows, preferred_element_type=jnp.float32)
    kv_grad = jnp.concatenate(
        [
            key_grad.reshape(flat_rows, key_value_columns),
            value_grad.reshape(flat_rows, key_value_columns),
        ],
        axis=1,
    ).astype(jnp.bfloat16)
    backward_piece = adapter_scale * jnp.concatenate(
        [
            lax.dot_general(
                kv_grad[:, :key_value_columns],
                adapter_up_weight[0, 0],
                contracted_columns,
                preferred_element_type=jnp.float32,
            ),
            lax.dot_general(
                kv_grad[:, key_value_columns:],
                adapter_up_weight[0, 1],
                contracted_columns,
                preferred_element_type=jnp.float32,
            ),
        ],
        axis=1,
    )
    backward_lowrank = lax.psum(backward_piece, "mp").astype(jnp.bfloat16)
    up_gradient = adapter_scale * jnp.stack(
        [
            lax.dot_general(
                lowrank_projection[:, :lowrank_state],
                kv_grad[:, :key_value_columns],
                contract_rows,
                preferred_element_type=jnp.float32,
            ),
            lax.dot_general(
                lowrank_projection[:, lowrank_state:],
                kv_grad[:, key_value_columns:],
                contract_rows,
                preferred_element_type=jnp.float32,
            ),
        ]
    )
    grad_down = lax.dot_general(
        image_fourth, backward_lowrank, contract_rows, preferred_element_type=jnp.float32
    )
    down_sum, up_sum = lax.psum((grad_down, up_gradient), "dp")
    image_gradient_total = lax.dot_general(
        kv_grad, full_weight, contracted_columns, preferred_element_type=jnp.float32
    )
    adapter_portion = lax.dot_general(
        backward_lowrank,
        adapter_down_weight[0],
        contracted_columns,
        preferred_element_type=jnp.float32,
    )
    current_layer = lax.dynamic_slice_in_dim(
        image_gradient_total, parallel_index * fourth_part, fourth_part, 1
    )
    image_gradient_total = lax.dynamic_update_slice_in_dim(
        image_gradient_total, current_layer + adapter_portion, parallel_index * fourth_part, 1
    )
    image_gradient_total = image_gradient_total.reshape(samples, image_rows, model_width)
    shared_sum = lax.psum_scatter(image_gradient_total, "segment", scatter_dimension=1, tiled=True)
    result = lax.psum(shared_sum, "mp")
    return (down_sum.astype(jnp.bfloat16)[None], up_sum.astype(jnp.bfloat16)[None], result)


def solution(mesh):
    in_specs = (
        P("dp", "segment", None),
        P("segment", "dp", None, "mp"),
        P("segment", "mp", None),
        P("segment", None, None, "mp"),
        P("segment", "dp", None, "mp"),
        P("segment", "dp", None, "mp"),
        P("dp"),
        P("dp"),
    )
    out_specs = (P("segment", "mp", None), P("segment", None, None, "mp"), P("dp", "segment", None))
    return jax.shard_map(body, mesh=mesh, in_specs=in_specs, out_specs=out_specs, check_vma=False)
```

profile of v0, /device:TPU:2, one launch (start us, length us, event | category | flops | bytes accessed | tf_op | source)
XLA Modules:
  0.0 390.2 jit_solution(4577795114373816345)
XLA Ops:
  7.2 0.7 all-gather.4.cloned.1.call-update
  8.0 0.7 all-gather.6.cloned.1.call-update
  10.0 1.3 copy.38
  11.3 2.0 copy.39
  13.4 88.8 %all-gather.4.cloned.1.call-done = bf16[1,128,8192]{2,1,0:T(8,128)(2,1)} async-done(((bf16[1,8,8192]{2,1,0:T(8,128)(2,1)}), bf16[1,128,8192]{2,1,0:T(8,128)(2,1)}) %all-gather.4.cloned.1.call-update) | async-done | bytes 2097168 | tf_op jit(solution)/shard_map/all_gather | solution.py:25
  102.2 1.3 fusion.21
  103.6 25.9 %psum.35 = bf16[128,128]{1,0:T(8,128)(2,1)S(1)} all-reduce(f32[128,128]{1,0:T(8,128)S(1)} %fusion.21), channel_id=1, replica_groups=mesh['segment'=16,'dp'=8,'mp'=4] {'mp'}, use_global_device_ids=true, to_apply=%region_0.0 | all-reduce | flops 16384 | bytes 98304 | tf_op jit(solution)/shard_map/psum | solution.py:34
  129.5 0.2 fusion.42
  129.7 0.1 fusion.46
  129.8 30.6 %all-gather.6.cloned.1.call-done = bf16[1,8192,2,256]{3,2,0,1:T(2,128)(2,1)} async-done(((bf16[1,1024,2,256]{3,2,0,1:T(2,128)(2,1)}), bf16[1,8192,2,256]{3,2,0,1:T(2,128)(2,1)}) %all-gather.6.cloned.1.call-update) | async-done | bytes 8388624 | tf_op jit(solution)/shard_map/all_gather | solution.py:53
  160.5 8.2 %copy.40 = bf16[1024,8,2,256]{3,1,2,0:T(8,128)(2,1)} copy(bf16[1024,8,2,256]{3,2,1,0:T(2,128)(2,1)} %bitcast.113) | data formatting | bytes 16777216
  168.6 4.6 %fusion.10 = bf16[128,512]{1,0:T(8,128)(2,1)S(1)} fusion(bf16[8192,512]{1,0:T(8,128)(2,1)} %bitcast.108, bf16[1,128,8192]{2,1,0:T(8,128)(2,1)S(1)} %copy-done.1, f32[128,256]{1,0:T(8,128)S(1)} %fusion.42, f32[128,256]{1,0:T(8,128)S(1)} %fusion.46), kind=kOutput, calls=%fused_computation.11 | convolution fusion | flops 1074003968 | bytes 10878976 | tf_op jit(solution)/shard_map/dot_general | solution.py:56
  173.3 0.3 fusion.66
  173.6 0.2 fusion.16
  173.8 1.6 fusion.14
  175.4 0.1 fusion.40
  175.6 0.3 multiply_reduce_fusion
  175.9 0.5 fusion.13
  176.4 1.5 slice-done.1
  177.9 4.8 %fusion.34 = f32[128,8192]{1,0:T(8,128)} fusion(bf16[8192,512]{1,0:T(8,128)(2,1)S(1)} %bitcast.111, bf16[128,256]{0,1:T(8,128)(2,1)S(1)} %bitcast.118, bf16[128,256]{0,1:T(8,128)(2,1)S(1)} %bitcast.120), kind=kOutput, calls=%fused_computation.42 | convolution fusion | flops 1074003968 | bytes 12713984 | tf_op jit(solution)/shard_map/dot_general | solution.py:135
  182.7 0.1 fusion.44
  182.8 26.9 %psum.36 = bf16[128,128]{0,1:T(8,128)(2,1)S(1)} all-reduce(f32[128,128]{0,1:T(8,128)S(1)} %maximum_multiply_fusion.2), channel_id=1, replica_groups=mesh['segment'=16,'dp'=8,'mp'=4] {'mp'}, use_global_device_ids=true, to_apply=%region_4.5 | all-reduce | flops 16384 | bytes 98304 | tf_op jit(solution)/shard_map/psum | solution.py:114
  209.8 4.6 %copy.51 = f32[1,128,8192]{2,1,0:T(8,128)} copy(f32[1,128,8192]{2,1,0:T(8,128)} %bitcast.112) | data formatting | bytes 8388608
  214.3 2.5 fusion.1
  216.8 0.0 all-reduce.4.cloned.1.call-start
  216.9 1.3 fusion.23
  218.2 0.2 convolution_bitcast_fusion.3
  218.4 0.2 convolution_bitcast_fusion.4
  218.7 89.1 %reduce-scatter.2.cloned.1.call-done = f32[1,8,8192]{2,1,0:T(8,128)} async-done(((f32[1,128,8192]{2,1,0:T(8,128)}), f32[1,8,8192]{2,1,0:T(8,128)}) %reduce-scatter.2.cloned.1.call-update) | async-done | bytes 262160 | tf_op jit(solution)/shard_map/reduce_scatter | solution.py:151
  307.7 52.3 %all-reduce.5 = (bf16[2048,128]{1,0:T(8,128)(2,1)}, bf16[2,64,256]{2,1,0:T(8,128)(2,1)}) all-reduce(f32[2048,128]{1,0:T(8,128)} %fusion.23, f32[2,64,256]{2,1,0:T(8,128)S(1)} %maximum_multiply_fusion.1), channel_id=1, replica_groups=mesh['segment'=16,'dp'=8,'mp'=4] {'dp'}, use_global_device_ids=true, to_apply=%region_5.6 | all-reduce | flops 294912 | bytes 1769472 | tf_op jit(solution)/shard_map/psum | solution.py:134
  360.0 22.0 %all-reduce.4.cloned.1.call-done = f32[1,8,8192]{2,1,0:T(8,128)} async-done(((f32[1,8,8192]{2,1,0:T(8,128)}), f32[1,8,8192]{2,1,0:T(8,128)}) %all-reduce.4.cloned.1.call-update) | async-done | bytes 262160 | tf_op jit(solution)/shard_map/psum | solution.py:152
  382.0 1.7 copy.57
  (24 shorter events, 0.3 us)
Async XLA Ops:
  7.2 95.1 %copy-start = (bf16[1,2048,128]{2,1,0:T(8,128)(2,1)S(1)}, bf16[1,2048,128]{2,1,0:T(8,128)(2,1)}, u32[]{:S(2)}) copy-start(bf16[1,2048,128]{2,1,0:T(8,128)(2,1)} %param.10) | copy-start | bytes 1572868
  7.2 122.3 %copy-start.3 = (bf16[1,2,64,256]{3,2,1,0:T(8,128)(2,1)S(1)}, bf16[1,2,64,256]{3,2,1,0:T(8,128)(2,1)}, u32[]{:S(2)}) copy-start(bf16[1,2,64,256]{3,2,1,0:T(8,128)(2,1)} %param.11) | copy-start | bytes 196612
  7.2 95.0 %all-gather.4.cloned.1.call-start = ((), (), s32[]{:S(2)}) async-start(), calls=%async_computation.1 | async-start | bytes 2228224 | tf_op jit(solution)/shard_map/all_gather | solution.py:25
  7.9 152.5 %all-gather.6.cloned.1.call-start = ((), (), s32[]{:S(2)}) async-start(), calls=%async_computation.4 | async-start | bytes 9437184 | tf_op jit(solution)/shard_map/all_gather | solution.py:53
  8.7 299.0 %reduce-scatter.2.cloned.1.call-start = ((), (), s32[]{:S(2)}) async-start(), calls=%async_computation.2 | async-start | bytes 4456448 | tf_op jit(solution)/shard_map/reduce_scatter | solution.py:151
  160.5 8.2 %copy-start.1 = (bf16[1,128,8192]{2,1,0:T(8,128)(2,1)S(1)}, bf16[1,128,8192]{2,1,0:T(8,128)(2,1)}, u32[]{:S(2)}) copy-start(bf16[1,128,8192]{2,1,0:T(8,128)(2,1)} %all-gather.4.cloned.1.call-done) | copy-start | bytes 6291460
  173.3 2.2 copy-start.2
  173.8 2.6 slice-start
  175.6 2.4 slice-start.1
  216.8 165.2 %all-reduce.4.cloned.1.call-start = ((), (), s32[]{:S(2)}) async-start(), calls=%async_computation.3 | async-start | bytes 524288 | tf_op jit(solution)/shard_map/psum | solution.py:152
Sparse Core Ops, SparseCore 0:
  10.1 92.1 all-gather.3
  104.4 56.0 all-gather.5
  217.0 90.7 reduce-scatter.1
  310.5 71.4 all-reduce.3
where the time goes:
time: 391 us; the launch traced here: 390 us
  waiting for transfers between devices  232 us (59%)
  blocking collectives  105 us (27%)
  local copies, waits for them, and re-layouts  19.3 us (5%)
  matrix products  18.3 us (5%)
  between operations  15.2 us (4%)
    reduce_scatter x1, waiting for transfers between devices, body(): lax.psum_scatter(image_gradient_total, 'segment', scatter_dimension=1, ti...  89.1 us
    all_gather x1, waiting for transfers between devices, body(): lax.all_gather(encoder_image_states, 'segment', axis=1, tiled=True)  88.8 us
    psum x1, blocking collectives, body(): down_sum, up_sum = lax.psum((grad_down, up_gradient), 'dp')  52.3 us
    all_gather x1, waiting for transfers between devices, body(): lax.all_gather(local_weight, 'dp', axis=0, tiled=True)  30.6 us
    psum x1, blocking collectives, body(): backward_lowrank = lax.psum(backward_piece, 'mp').astype(jnp.bfloat16)  26.9 us
    psum x1, blocking collectives, body(): lax.psum(jnp.dot(image_fourth, adapter_down_weight[0], preferred_element_...  25.9 us
    psum x1, waiting for transfers between devices, body(): result = lax.psum(shared_sum, 'mp')  22 us
    unnamed x15, local copies, waits for them, and re-layouts  15.9 us
  transfers between devices with their start and end apart: 4, of which 4 were waited for; matrix products, arithmetic and copies ran while one was open for 2% of the time, Pallas kernels for 0%

commit v1 on v0

--- a/solution.py
+++ b/solution.py
@@ -149,7 +149,7 @@
     )
     image_gradient_total = image_gradient_total.reshape(samples, image_rows, model_width)
     shared_sum = lax.psum_scatter(image_gradient_total, "segment", scatter_dimension=1, tiled=True)
-    result = lax.psum(shared_sum, "mp")
+    result = jnp.sum(lax.all_gather(shared_sum, axis_name="mp"), 0)
     return (down_sum.astype(jnp.bfloat16)[None], up_sum.astype(jnp.bfloat16)[None], result)
 
 

time: 391 us -> 381 us (0.974)
  the two profiles are of different devices: /device:TPU:2 before, /device:TPU:1 now
where the time goes in v1:
time: 381 us
  waiting for transfers between devices  218 us (57%)
  blocking collectives  109 us (29%)
  matrix products  18.3 us (5%)
  local copies, waits for them, and re-layouts  17.6 us (5%)
  between operations  15.2 us (4%)
    reduce_scatter x1, waiting for transfers between devices, body(): lax.psum_scatter(image_gradient_total, 'segment', scatter_dimension=1, ti...  87.5 us
    all_gather x1, waiting for transfers between devices, body(): lax.all_gather(encoder_image_states, 'segment', axis=1, tiled=True)  79.7 us
    psum x1, blocking collectives, body(): down_sum, up_sum = lax.psum((grad_down, up_gradient), 'dp')  62.8 us
    all_gather x1, waiting for transfers between devices, body(): lax.all_gather(local_weight, 'dp', axis=0, tiled=True)  44.3 us
    psum x1, blocking collectives, body(): backward_lowrank = lax.psum(backward_piece, 'mp').astype(jnp.bfloat16)  23.9 us
    psum x1, blocking collectives, body(): lax.psum(jnp.dot(image_fourth, adapter_down_weight[0], preferred_element_...  22.6 us
    unnamed x14, local copies, waits for them, and re-layouts  14.2 us
  transfers between devices with their start and end apart: 4, of which 4 were waited for; matrix products, arithmetic and copies ran while one was open for 2% of the time, Pallas kernels for 0%

profile of v1, /device:TPU:1, one launch (start us, length us, event | category | flops | bytes accessed | tf_op | source)
XLA Modules:
  0.0 380.7 jit_solution(15548721168557322286)
XLA Ops:
  7.2 0.7 all-gather.6.cloned.1.call-update
  8.0 0.7 all-gather.8.cloned.1.call-update
  10.0 1.3 copy.38
  11.3 2.0 copy.39
  13.4 79.7 %all-gather.6.cloned.1.call-done = bf16[1,128,8192]{2,1,0:T(8,128)(2,1)} async-done(((bf16[1,8,8192]{2,1,0:T(8,128)(2,1)}), bf16[1,128,8192]{2,1,0:T(8,128)(2,1)}) %all-gather.6.cloned.1.call-update) | async-done | bytes 2097168 | tf_op jit(solution)/shard_map/all_gather | solution.py:25
  93.1 1.3 fusion.21
  94.5 22.6 %psum.28 = bf16[128,128]{1,0:T(8,128)(2,1)S(1)} all-reduce(f32[128,128]{1,0:T(8,128)S(1)} %fusion.21), channel_id=1, replica_groups=mesh['segment'=16,'dp'=8,'mp'=4] {'mp'}, use_global_device_ids=true, to_apply=%region_0.0 | all-reduce | flops 16384 | bytes 98304 | tf_op jit(solution)/shard_map/psum | solution.py:34
  117.1 0.2 fusion.42
  117.3 0.1 fusion.46
  117.4 44.3 %all-gather.8.cloned.1.call-done = bf16[1,8192,2,256]{3,2,0,1:T(2,128)(2,1)} async-done(((bf16[1,1024,2,256]{3,2,0,1:T(2,128)(2,1)}), bf16[1,8192,2,256]{3,2,0,1:T(2,128)(2,1)}) %all-gather.8.cloned.1.call-update) | async-done | bytes 8388624 | tf_op jit(solution)/shard_map/all_gather | solution.py:53
  161.7 8.2 %copy.40 = bf16[1024,8,2,256]{3,1,2,0:T(8,128)(2,1)} copy(bf16[1024,8,2,256]{3,2,1,0:T(2,128)(2,1)} %bitcast.114) | data formatting | bytes 16777216
  169.9 4.6 %fusion.10 = bf16[128,512]{1,0:T(8,128)(2,1)S(1)} fusion(bf16[8192,512]{1,0:T(8,128)(2,1)} %bitcast.109, bf16[1,128,8192]{2,1,0:T(8,128)(2,1)S(1)} %copy-done.1, f32[128,256]{1,0:T(8,128)S(1)} %fusion.42, f32[128,256]{1,0:T(8,128)S(1)} %fusion.46), kind=kOutput, calls=%fused_computation.11 | convolution fusion | flops 1074003968 | bytes 10878976 | tf_op jit(solution)/shard_map/dot_general | solution.py:56
  174.6 0.3 fusion.66
  174.9 0.2 fusion.16
  175.1 1.6 fusion.14
  176.7 0.1 fusion.40
  176.8 0.3 multiply_reduce_fusion
  177.2 0.5 fusion.13
  177.7 1.5 slice-done.1
  179.2 4.8 %fusion.34 = f32[128,8192]{1,0:T(8,128)} fusion(bf16[8192,512]{1,0:T(8,128)(2,1)S(1)} %bitcast.112, bf16[128,256]{0,1:T(8,128)(2,1)S(1)} %bitcast.119, bf16[128,256]{0,1:T(8,128)(2,1)S(1)} %bitcast.121), kind=kOutput, calls=%fused_computation.42 | convolution fusion | flops 1074003968 | bytes 12713984 | tf_op jit(solution)/shard_map/dot_general | solution.py:135
  183.9 0.1 fusion.44
  184.1 23.9 %psum.29 = bf16[128,128]{0,1:T(8,128)(2,1)S(1)} all-reduce(f32[128,128]{0,1:T(8,128)S(1)} %maximum_multiply_fusion.2), channel_id=1, replica_groups=mesh['segment'=16,'dp'=8,'mp'=4] {'mp'}, use_global_device_ids=true, to_apply=%region_4.5 | all-reduce | flops 16384 | bytes 98304 | tf_op jit(solution)/shard_map/psum | solution.py:114
  208.0 4.6 %copy.51 = f32[1,128,8192]{2,1,0:T(8,128)} copy(f32[1,128,8192]{2,1,0:T(8,128)} %bitcast.113) | data formatting | bytes 8388608
  212.6 2.5 fusion.1
  215.1 0.0 all-gather.10.cloned.1.call-start
  215.1 87.5 %reduce-scatter.2.cloned.1.call-done = f32[1,8,8192]{2,1,0:T(8,128)} async-done(((f32[1,128,8192]{2,1,0:T(8,128)}), f32[1,8,8192]{2,1,0:T(8,128)}) %reduce-scatter.2.cloned.1.call-update) | async-done | bytes 262160 | tf_op jit(solution)/shard_map/reduce_scatter | solution.py:151
  302.7 1.4 fusion.23
  304.1 0.2 convolution_bitcast_fusion.3
  304.3 0.2 convolution_bitcast_fusion.4
  304.5 62.8 %all-reduce.2 = (bf16[2048,128]{1,0:T(8,128)(2,1)}, bf16[2,64,256]{2,1,0:T(8,128)(2,1)}) all-reduce(f32[2048,128]{1,0:T(8,128)} %fusion.23, f32[2,64,256]{2,1,0:T(8,128)S(1)} %maximum_multiply_fusion.1), channel_id=1, replica_groups=mesh['segment'=16,'dp'=8,'mp'=4] {'dp'}, use_global_device_ids=true, to_apply=%region_5.6 | all-reduce | flops 294912 | bytes 1769472 | tf_op jit(solution)/shard_map/psum | solution.py:134
  367.3 4.8 %all-gather.10.cloned.1.call-done = f32[4,8,8192]{2,1,0:T(8,128)} async-done(((f32[1,8,8192]{2,1,0:T(8,128)}), f32[4,8,8192]{2,1,0:T(8,128)}) %all-gather.10.cloned.1.call-update) | async-done | bytes 1048592 | tf_op jit(solution)/shard_map/all_gather | solution.py:152
  372.2 2.0 reduce.4
  (24 shorter events, 0.3 us)
Async XLA Ops:
  7.2 86.0 %copy-start = (bf16[1,2048,128]{2,1,0:T(8,128)(2,1)S(1)}, bf16[1,2048,128]{2,1,0:T(8,128)(2,1)}, u32[]{:S(2)}) copy-start(bf16[1,2048,128]{2,1,0:T(8,128)(2,1)} %param.10) | copy-start | bytes 1572868
  7.2 109.9 %copy-start.3 = (bf16[1,2,64,256]{3,2,1,0:T(8,128)(2,1)S(1)}, bf16[1,2,64,256]{3,2,1,0:T(8,128)(2,1)}, u32[]{:S(2)}) copy-start(bf16[1,2,64,256]{3,2,1,0:T(8,128)(2,1)} %param.11) | copy-start | bytes 196612
  7.2 85.9 %all-gather.6.cloned.1.call-start = ((), (), s32[]{:S(2)}) async-start(), calls=%async_computation.1 | async-start | bytes 2228224 | tf_op jit(solution)/shard_map/all_gather | solution.py:25
  7.9 153.8 %all-gather.8.cloned.1.call-start = ((), (), s32[]{:S(2)}) async-start(), calls=%async_computation.3 | async-start | bytes 9437184 | tf_op jit(solution)/shard_map/all_gather | solution.py:53
  8.7 294.0 %reduce-scatter.2.cloned.1.call-start = ((), (), s32[]{:S(2)}) async-start(), calls=%async_computation.2 | async-start | bytes 4456448 | tf_op jit(solution)/shard_map/reduce_scatter | solution.py:151
  161.7 8.2 %copy-start.1 = (bf16[1,128,8192]{2,1,0:T(8,128)(2,1)S(1)}, bf16[1,128,8192]{2,1,0:T(8,128)(2,1)}, u32[]{:S(2)}) copy-start(bf16[1,128,8192]{2,1,0:T(8,128)(2,1)} %all-gather.6.cloned.1.call-done) | copy-start | bytes 6291460
  174.6 2.2 copy-start.2
  175.1 2.6 slice-start
  176.8 2.4 slice-start.1
  215.1 157.1 %all-gather.10.cloned.1.call-start = ((), (), s32[]{:S(2)}) async-start(), calls=%async_computation.4 | async-start | bytes 1310720 | tf_op jit(solution)/shard_map/all_gather | solution.py:152
Sparse Core Ops, SparseCore 0:
  10.1 83.0 all-gather.5
  95.3 66.3 all-gather.7
  215.2 87.4 reduce-scatter.1
  304.6 67.4 all-gather.9
